TPU v7x, 32 devices: a whole 2x2x4 slice. The times are simulated.
32 devices in a mesh: row: 8 (over y, x, core), col: 4 (over z).
Axes of the slice: x: 2, y: 2, z: 4, core: 2. Of those that a mesh axis runs over, the one named last changes fastest.
Arguments:
- panel: bfloat16 [24576, 256], P('row', 'col'), as said below
- trailing: bfloat16 [24576, 16384], P('row', 'col'), may hold values from -6 to 6
- tile_list: int32 [176], P('row'), may hold values from 0 to 23, as said below
Outputs:
- triangle: float32 [256, 256], replicated
- top_rows: float32 [16384, 256], P('col')
- updated: bfloat16 [22528, 16384], P('row', 'col')
Inputs may be any that keep to these rules, and one draw needn't show every extreme that they name: `tile_list`: each aligned block of 22 entries (the entries of one index of row) lists distinct tile numbers of that group's 24 tiles in increasing order and always includes tile 24 - 1. `panel`: the active rows of every row group, and all active rows together, have full column rank with a condition number under 100.
All inputs are finite; a program needn't handle non-finite values.
Results may differ from a plain program's by a relative error of at most 0.0065.
Values may be sent and summed in bfloat16 or wider, within the bound.
No kernel may reach another device: no remote copies, remote signals or barrier semaphores. Data moves between devices by JAX's collectives and lax.ppermute only.
A program may use at most 128 MiB of HBM per device.

v0:
```python
import jax
import jax.numpy as jnp
from jax import lax
from jax.sharding import PartitionSpec as P

TILE = 128


def pick_tiles(whole, tile_list):
    tiled = whole.reshape(-1, TILE, whole.shape[1])
    return jnp.take(tiled, tile_list, axis=0).reshape(-1, whole.shape[1])


def local(panel, trailing, tile_list):
    panel_full = lax.all_gather(panel, "col", axis=1, tiled=True)
    act_panel = pick_tiles(panel_full, tile_list)
    act_trail = pick_tiles(trailing, tile_list)
    local_gram = lax.dot_general(
        act_panel, act_panel, (((0,), (0,)), ((), ())), preferred_element_type=jnp.float32
    )
    gram_matrix = lax.psum(local_gram.astype(jnp.bfloat16), "row").astype(jnp.float32)
    lower_factor = jnp.linalg.cholesky(gram_matrix)
    triangle = lower_factor.T
    local_cross = lax.dot_general(
        act_trail, act_panel, (((0,), (0,)), ((), ())), preferred_element_type=jnp.float32
    )
    cross_sum = lax.psum(local_cross, "row")
    top_rows = jax.scipy.linalg.solve_triangular(lower_factor, cross_sum.T, lower=True).T
    coeff = jax.scipy.linalg.solve_triangular(
        lower_factor, top_rows.T, lower=True, trans=1
    ).T.astype(jnp.bfloat16)
    product = lax.dot_general(
        act_panel, coeff, (((1,), (1,)), ((), ())), preferred_element_type=jnp.float32
    )
    updated = (act_trail.astype(jnp.float32) - product).astype(jnp.bfloat16)
    return (triangle, top_rows, updated)


def solution(mesh):
    return jax.shard_map(
        local,
        mesh=mesh,
        in_specs=(P("row", "col"), P("row", "col"), P("row")),
        out_specs=(P(), P("col", None), P("row", "col")),
        check_vma=False,
    )
```

profile of v0, /device:TPU:0, one launch (start us, length us, event | category | flops | bytes accessed | tf_op | source)
XLA Modules:
  0.0 239.5 jit_solution(15465657170109536758)
XLA Ops:
  7.2 0.0 all-gather.2.cloned.1.call-start
  7.2 0.7 all-gather.2.cloned.1.call-update
  7.9 0.0 all-reduce.4.cloned.1.call-start
  7.9 0.7 compare_and_fusion
  8.6 0.7 compare_select_fusion
  9.3 0.1 broadcast_bitcast_fusion
  9.4 17.7 %gather_fusion.1 = bf16[22,128,4096]{2,1,0:T(8,128)(2,1)} fusion(bf16[24,128,4096]{2,1,0:T(8,128)(2,1)} %bitcast.57, s32[1024]{0:T(1024)S(1)} %pad_clamp_fusion), kind=kCustom, calls=%fused_computation.1 | custom fusion | bytes 46137432 | tf_op jit(solution)/shard_map/jit(_take)/gather | solution.py:11
  27.1 20.6 %bitcast_select_fusion = bf16[2816,4096]{1,0:T(8,128)(2,1)} fusion(bf16[22,128,4096]{2,1,0:T(8,128)(2,1)} %gather_fusion.1, pred[2816]{0:T(1024)(128)(4,1)S(1)} %broadcast_bitcast_fusion), kind=kLoop, calls=%fused_computation.5 | loop fusion | flops 11534336 | bytes 46140160 | tf_op jit(solution)/shard_map/jit(_take)/select_n | solution.py:11
  47.7 1.6 all-gather.2.cloned.1.call-done
  49.3 1.7 copy.11
  51.0 0.6 gather_fusion
  51.7 1.5 fusion.12
  53.1 0.0 all-reduce.4.cloned.1.call-update
  53.2 0.0 all-reduce.6.cloned.1.call-start
  53.2 12.2 %fusion.4 = f32[256,4096]{1,0:T(8,128)} fusion(bf16[22,128,4096]{2,1,0:T(8,128)(2,1)} %gather_fusion.1, pred[22]{0:T(512)(128)(4,1)S(1)} %compare_and_fusion, bf16[22,128,256]{2,1,0:T(8,128)(2,1)S(1)} %gather_fusion), kind=kOutput, calls=%fused_computation.10 | convolution fusion | flops 5917835264 | bytes 28704790 | tf_op jit(solution)/shard_map/dot_general | solution.py:24
  65.4 0.0 all-reduce.6.cloned.1.call-update
  65.4 1.7 bitcast_select_fusion.1
  67.1 40.8 %all-reduce.4.cloned.1.call-done = bf16[256,256]{0,1:T(8,128)(2,1)} async-done(((bf16[256,256]{0,1:T(8,128)(2,1)}), bf16[256,256]{0,1:T(8,128)(2,1)}) %all-reduce.4.cloned.1.call-update) | async-done | bytes 131088 | tf_op jit(solution)/shard_map/psum | solution.py:21
  107.9 1.0 copy.14
  108.9 0.9 fusion.13
  109.9 11.7 %cholesky.50 = f32[128,128]{1,0:T(8,128)S(1)} custom-call(f32[128,128]{1,0:T(8,128)S(1)} %cholesky.118), custom_call_target="Cholesky" | custom-call | tf_op jit(solution)/shard_map/jit(cholesky)/cholesky | solution.py:22
  121.6 9.8 %custom-call.18 = f32[1,128,128]{1,2,0:T(8,128)S(1)} custom-call(f32[1,128,128]{2,1,0:T(8,128)S(1)} %get-tuple-element.32), custom_call_target="InvertDiagBlocksLowerTriangular" | custom-call | tf_op jit(solution)/shard_map/jit(cholesky)/cholesky | solution.py:22
  131.5 0.2 constant_dynamic-update-slice_fusion.1
  131.7 0.3 convolution_subtract_fusion.2
  131.9 11.7 %cholesky.105 = f32[128,128]{1,0:T(8,128)S(1)} custom-call(f32[128,128]{1,0:T(8,128)S(1)} %convolution_subtract_fusion.2), custom_call_target="Cholesky" | custom-call | tf_op jit(solution)/shard_map/jit(cholesky)/cholesky | solution.py:22
  143.7 0.6 compare_reduce_fusion
  145.7 0.8 copy.16
  146.5 0.1 triangular_solve.53
  146.6 4.0 %while.1 = (s32[]{:T(128)}, f32[256,256]{1,0:T(8,128)S(1)}, s32[2,2]{1,0:T(2,128)S(1)}, f32[2,128,128]{2,1,0:T(8,128)S(1)}, s32[]{:T(128)}) while((s32[]{:T(128)}, f32[256,256]{1,0:T(8,128)S(1)}, s32[2,2]{1,0:T(2,128)S(1)}, f32[2,128,128]{2,1,0:T(8,128)S(1)}, s32[]{:T(128)}) %tuple.31), condition=%wide.while_cond, body=%wide.while_body.sunk | while | flops 2 | bytes 131189 | solution.py:28
  146.6 0.6 fusion.37
  147.2 1.4 bitcast_dynamic-update-slice_fusion.2
  148.6 0.6 fusion.37
  149.2 1.4 bitcast_dynamic-update-slice_fusion.2
  150.6 19.9 %custom-call.19 = f32[2,128,128]{1,2,0:T(8,128)S(1)} custom-call(f32[2,128,128]{2,1,0:T(8,128)S(1)} %get-tuple-element.10), custom_call_target="InvertDiagBlocksLowerTriangular" | custom-call | tf_op jit(solution)/shard_map/jit(_solve_triangular)/triangular_solve | solution.py:28
  170.5 0.0 copy-start.1
  170.5 21.7 %all-reduce.6.cloned.1.call-done = f32[256,4096]{1,0:T(8,128)} async-done(((f32[256,4096]{1,0:T(8,128)}), f32[256,4096]{1,0:T(8,128)}) %all-reduce.6.cloned.1.call-update) | async-done | bytes 4194320 | tf_op jit(solution)/shard_map/psum | solution.py:27
  192.2 3.6 %fusion.7 = f32[128,4096]{1,0:T(8,128)S(1)} fusion(f32[256,4096]{1,0:T(8,128)} %all-reduce.6.cloned.1.call-done, f32[2,128,128]{1,2,0:T(8,128)S(1)} %custom-call.19), kind=kOutput, calls=%fused_computation.15 | convolution fusion | flops 805306368 | bytes 4259840 | tf_op jit(solution)/shard_map/jit(_solve_triangular)/triangular_solve | solution.py:28
  195.9 0.0 copy-done
  195.9 1.9 convolution_subtract_fusion.1
  197.8 1.9 fusion.20
  199.8 0.0 copy-done.1
  199.8 1.9 fusion.27
  201.7 2.5 %maximum_bitcast_fusion = f32[4096,256]{0,1:T(8,128)} fusion(f32[128,4096]{1,0:T(8,128)S(1)} %fusion.20, f32[128,4096]{1,0:T(8,128)S(1)} %fusion.7), kind=kLoop, calls=%fused_computation.14 | loop fusion | flops 1048576 | bytes 8388608 | tf_op jit(solution)/shard_map/transpose | solution.py:28
  204.2 2.0 convolution_subtract_fusion
  206.1 0.0 copy-done.2
  206.2 1.9 convolution_convert_fusion
  208.1 5.9 %copy.17 = f32[4096,256]{1,0:T(8,128)} copy(f32[4096,256]{0,1:T(8,128)} %maximum_bitcast_fusion) | data formatting | bytes 8388608
  213.9 19.1 %subtract_convert_fusion = bf16[2816,4096]{1,0:T(8,128)(2,1)} fusion(bf16[2816,4096]{1,0:T(8,128)(2,1)} %bitcast_select_fusion, bf16[2816,256]{1,0:T(8,128)(2,1)S(1)} %bitcast_select_fusion.1, bf16[128,4096]{1,0:T(8,128)(2,1)S(1)} %get-tuple-element.35, bf16[128,4096]{1,0:T(8,128)(2,1)S(1)} %convolution_convert_fusion), kind=kOutput, calls=%fused_computation.4 | convolution fusion | flops 5944377344 | bytes 49676288 | tf_op jit(solution)/shard_map/dot_general | solution.py:32
  (12 shorter events, 0.2 us)
Async XLA Ops:
  7.2 42.2 %all-gather.2.cloned.1.call-start = ((), (), s32[]{:S(2)}) async-start(), calls=%async_computation | async-start | bytes 1966080 | tf_op jit(solution)/shard_map/all_gather | solution.py:15
  7.9 100.0 %all-reduce.4.cloned.1.call-start = ((), (), s32[]{:S(2)}) async-start(), calls=%async_computation.1 | async-start | bytes 262144 | tf_op jit(solution)/shard_map/psum | solution.py:21
  53.2 139.0 %all-reduce.6.cloned.1.call-start = ((), (), s32[]{:S(2)}) async-start(), calls=%async_computation.2 | async-start | bytes 8388608 | tf_op jit(solution)/shard_map/psum | solution.py:27
  170.5 29.2 %copy-start.1 = (f32[2,128,128]{1,2,0:T(8,128)}, f32[2,128,128]{1,2,0:T(8,128)S(1)}, u32[]{:S(2)}) copy-start(f32[2,128,128]{1,2,0:T(8,128)S(1)} %custom-call.19) | copy-start | bytes 393220
  192.2 3.7 %copy-start = (f32[256,4096]{1,0:T(8,128)S(1)}, f32[256,4096]{1,0:T(8,128)}, u32[]{:S(2)}) copy-start(f32[256,4096]{1,0:T(8,128)} %all-reduce.6.cloned.1.call-done) | copy-start | bytes 12582916
  204.2 2.0 copy-start.2
Sparse Core Ops, SparseCore 0:
  9.5 39.7 all-gather.1
  53.3 54.5 all-reduce.3
  111.7 80.4 all-reduce.5
where the time goes:
time: 240 us
  other arithmetic  80.9 us (34%)
  waiting for transfers between devices  64.8 us (27%)
  matrix products  46.5 us (19%)
  local copies, waits for them, and re-layouts  31.9 us (13%)
  between operations  15.2 us (6%)
    psum x1, waiting for transfers between devices, local(): lax.psum(local_gram.astype(jnp.bfloat16), 'row').astype(jnp.float32)  40.8 us
    another operation x6, other arithmetic, local(): lower_factor = jnp.linalg.cholesky(gram_matrix)  34 us
    select_n x3, other arithmetic, pick_tiles(): return jnp.take(tiled, tile_list, axis=0).reshape(-1, whole.shape[1])  22.9 us
    psum x1, waiting for transfers between devices, local(): cross_sum = lax.psum(local_cross, 'row')  21.7 us
    another operation x3, other arithmetic, local(): jax.scipy.linalg.solve_triangular(lower_factor, cross_sum.T, lower=True)  19.9 us
    dot_general x1, matrix products, local(): lax.dot_general(act_panel, coeff, (((1,), (1,)), ((), ())), preferred_ele...  19.1 us
    gather x2, local copies, waits for them, and re-layouts, pick_tiles(): return jnp.take(tiled, tile_list, axis=0).reshape(-1, whole.shape[1])  18.4 us
    dot_general x1, matrix products, local(): lax.dot_general(act_trail, act_panel, (((0,), (0,)), ((), ())), preferred...  12.2 us
  transfers between devices with their start and end apart: 3, of which 3 were waited for; matrix products, arithmetic and copies ran while one was open for 48% of the time, Pallas kernels for 0%

commit v1 on v0

--- a/solution.py
+++ b/solution.py
@@ -18,7 +18,8 @@
     local_gram = lax.dot_general(
         act_panel, act_panel, (((0,), (0,)), ((), ())), preferred_element_type=jnp.float32
     )
-    gram_matrix = lax.psum(local_gram.astype(jnp.bfloat16), "row").astype(jnp.float32)
+    produce_windows = lambda here_x, along_axis: jnp.sum(lax.all_gather(here_x, along_axis), axis=0)
+    gram_matrix = produce_windows(local_gram.astype(jnp.bfloat16), "row").astype(jnp.float32)
     lower_factor = jnp.linalg.cholesky(gram_matrix)
     triangle = lower_factor.T
     local_cross = lax.dot_general(

time: 240 us -> 211 us (0.88)
  waiting for transfers between devices: 64.8 us -> 35.7 us
    psum x1 -> x0, waiting for transfers between devices: 40.8 us -> none  [local(): lax.psum(local_gram.astype(jnp.bfloat16), 'row').astype(jnp.float32)]
    all_gather x0 -> x1, waiting for transfers between devices: none -> 10.8 us  [local(): lax.all_gather(here_x, along_axis)]
  transfers between devices with their start and end apart: 3 -> 3, of which waited for: 3 -> 3; matrix products, arithmetic and copies ran while one was open for 48% -> 54% of each run, Pallas kernels for 0% -> 0%
where the time goes in v1:
time: 211 us; the launch traced here: 210 us
  other arithmetic  81.4 us (39%)
  matrix products  46.5 us (22%)
  waiting for transfers between devices  35.7 us (17%)
  local copies, waits for them, and re-layouts  31.1 us (15%)
  between operations  15.2 us (7%)
    another operation x6, other arithmetic, local(): lower_factor = jnp.linalg.cholesky(gram_matrix)  34 us
    select_n x3, other arithmetic, pick_tiles(): return jnp.take(tiled, tile_list, axis=0).reshape(-1, whole.shape[1])  22.9 us
    psum x1, waiting for transfers between devices, local(): cross_sum = lax.psum(local_cross, 'row')  22.6 us
    another operation x3, other arithmetic, local(): jax.scipy.linalg.solve_triangular(lower_factor, cross_sum.T, lower=True)  19.9 us
    dot_general x1, matrix products, local(): lax.dot_general(act_panel, coeff, (((1,), (1,)), ((), ())), preferred_ele...  19.1 us
    gather x2, local copies, waits for them, and re-layouts, pick_tiles(): return jnp.take(tiled, tile_list, axis=0).reshape(-1, whole.shape[1])  18.4 us
    dot_general x1, matrix products, local(): lax.dot_general(act_trail, act_panel, (((0,), (0,)), ((), ())), preferred...  12.1 us
    all_gather x1, waiting for transfers between devices, local(): lax.all_gather(here_x, along_axis)  10.8 us
  transfers between devices with their start and end apart: 3, of which 3 were waited for; matrix products, arithmetic and copies ran while one was open for 54% of the time, Pallas kernels for 0%

profile of v1, /device:TPU:0, one launch (start us, length us, event | category | flops | bytes accessed | tf_op | source)
XLA Modules:
  0.0 210.2 jit_solution(8633984732473702305)
XLA Ops:
  7.2 0.0 all-gather.4.cloned.1.call-start
  7.2 0.7 all-gather.4.cloned.1.call-update
  7.9 0.0 all-gather.6.cloned.1.call-start
  7.9 0.7 compare_and_fusion
  8.6 0.7 compare_select_fusion
  9.3 0.1 broadcast_bitcast_fusion
  9.4 17.7 %gather_fusion.1 = bf16[22,128,4096]{2,1,0:T(8,128)(2,1)} fusion(bf16[24,128,4096]{2,1,0:T(8,128)(2,1)} %bitcast.58, s32[1024]{0:T(1024)S(1)} %pad_clamp_fusion), kind=kCustom, calls=%fused_computation.1 | custom fusion | bytes 46137432 | tf_op jit(solution)/shard_map/jit(_take)/gather | solution.py:11
  27.1 20.6 %bitcast_select_fusion = bf16[2816,4096]{1,0:T(8,128)(2,1)} fusion(bf16[22,128,4096]{2,1,0:T(8,128)(2,1)} %gather_fusion.1, pred[2816]{0:T(1024)(128)(4,1)S(1)} %broadcast_bitcast_fusion), kind=kLoop, calls=%fused_computation.5 | loop fusion | flops 11534336 | bytes 46140160 | tf_op jit(solution)/shard_map/jit(_take)/select_n | solution.py:11
  47.7 1.6 all-gather.4.cloned.1.call-done
  49.3 1.7 copy.16
  51.0 0.6 gather_fusion
  51.7 1.5 fusion.12
  53.2 0.0 all-gather.6.cloned.1.call-update
  53.2 0.0 all-reduce.3.cloned.1.call-start
  53.3 12.1 %fusion.4 = f32[256,4096]{1,0:T(8,128)} fusion(bf16[22,128,4096]{2,1,0:T(8,128)(2,1)} %gather_fusion.1, pred[22]{0:T(512)(128)(4,1)S(1)} %compare_and_fusion, bf16[22,128,256]{2,1,0:T(8,128)(2,1)S(1)} %gather_fusion), kind=kOutput, calls=%fused_computation.10 | convolution fusion | flops 5917835264 | bytes 28704790 | tf_op jit(solution)/shard_map/dot_general | solution.py:25
  65.4 0.0 all-reduce.3.cloned.1.call-update
  65.5 1.7 bitcast_select_fusion.1
  67.1 10.8 %all-gather.6.cloned.1.call-done = bf16[2048,256]{1,0:T(8,128)(2,1)} async-done(((bf16[256,256]{1,0:T(8,128)(2,1)}), bf16[2048,256]{1,0:T(8,128)(2,1)}) %all-gather.6.cloned.1.call-update) | async-done | bytes 1048592 | tf_op jit(solution)/shard_map/all_gather | solution.py:21
  77.9 1.4 reduce_sum.12
  79.3 0.1 copy.18
  79.4 0.1 copy.19
  79.5 11.7 %cholesky.50 = f32[128,128]{1,0:T(8,128)S(1)} custom-call(f32[128,128]{1,0:T(8,128)S(1)} %cholesky.118), custom_call_target="Cholesky" | custom-call | tf_op jit(solution)/shard_map/jit(cholesky)/cholesky | solution.py:23
  91.3 9.8 %custom-call.18 = f32[1,128,128]{1,2,0:T(8,128)S(1)} custom-call(f32[1,128,128]{2,1,0:T(8,128)S(1)} %get-tuple-element.35), custom_call_target="InvertDiagBlocksLowerTriangular" | custom-call | tf_op jit(solution)/shard_map/jit(cholesky)/cholesky | solution.py:23
  101.1 0.2 constant_dynamic-update-slice_fusion.1
  101.3 0.3 convolution_subtract_fusion.2
  101.6 11.7 %cholesky.105 = f32[128,128]{1,0:T(8,128)S(1)} custom-call(f32[128,128]{1,0:T(8,128)S(1)} %convolution_subtract_fusion.2), custom_call_target="Cholesky" | custom-call | tf_op jit(solution)/shard_map/jit(cholesky)/cholesky | solution.py:23
  113.3 0.6 compare_reduce_fusion
  115.3 0.8 copy.21
  116.2 0.1 triangular_solve.53
  116.2 4.0 %while.1 = (s32[]{:T(128)}, f32[256,256]{1,0:T(8,128)S(1)}, s32[2,2]{1,0:T(2,128)S(1)}, f32[2,128,128]{2,1,0:T(8,128)S(1)}, s32[]{:T(128)}) while((s32[]{:T(128)}, f32[256,256]{1,0:T(8,128)S(1)}, s32[2,2]{1,0:T(2,128)S(1)}, f32[2,128,128]{2,1,0:T(8,128)S(1)}, s32[]{:T(128)}) %tuple.32), condition=%wide.while_cond, body=%wide.while_body.sunk | while | flops 2 | bytes 131189 | solution.py:29
  116.2 0.6 fusion.37
  116.8 1.4 bitcast_dynamic-update-slice_fusion.2
  118.3 0.6 fusion.37
  118.9 1.4 bitcast_dynamic-update-slice_fusion.2
  120.3 19.9 %custom-call.19 = f32[2,128,128]{1,2,0:T(8,128)S(1)} custom-call(f32[2,128,128]{2,1,0:T(8,128)S(1)} %get-tuple-element.10), custom_call_target="InvertDiagBlocksLowerTriangular" | custom-call | tf_op jit(solution)/shard_map/jit(_solve_triangular)/triangular_solve | solution.py:29
  140.2 0.0 copy-start.1
  140.2 22.6 %all-reduce.3.cloned.1.call-done = f32[256,4096]{1,0:T(8,128)} async-done(((f32[256,4096]{1,0:T(8,128)}), f32[256,4096]{1,0:T(8,128)}) %all-reduce.3.cloned.1.call-update) | async-done | bytes 4194320 | tf_op jit(solution)/shard_map/psum | solution.py:28
  162.8 3.6 %fusion.7 = f32[128,4096]{1,0:T(8,128)S(1)} fusion(f32[256,4096]{1,0:T(8,128)} %all-reduce.3.cloned.1.call-done, f32[2,128,128]{1,2,0:T(8,128)S(1)} %custom-call.19), kind=kOutput, calls=%fused_computation.15 | convolution fusion | flops 805306368 | bytes 4259840 | tf_op jit(solution)/shard_map/jit(_solve_triangular)/triangular_solve | solution.py:29
  166.5 0.0 copy-done
  166.5 1.9 convolution_subtract_fusion.1
  168.4 1.9 fusion.20
  170.4 0.0 copy-done.1
  170.4 1.9 fusion.27
  172.3 2.5 %maximum_bitcast_fusion = f32[4096,256]{0,1:T(8,128)} fusion(f32[128,4096]{1,0:T(8,128)S(1)} %fusion.20, f32[128,4096]{1,0:T(8,128)S(1)} %fusion.7), kind=kLoop, calls=%fused_computation.14 | loop fusion | flops 1048576 | bytes 8388608 | tf_op jit(solution)/shard_map/transpose | solution.py:29
  174.8 2.0 convolution_subtract_fusion
  176.8 1.9 convolution_convert_fusion
  178.7 5.9 %copy.22 = f32[4096,256]{1,0:T(8,128)} copy(f32[4096,256]{0,1:T(8,128)} %maximum_bitcast_fusion) | data formatting | bytes 8388608
  184.6 19.1 %subtract_convert_fusion = bf16[2816,4096]{1,0:T(8,128)(2,1)} fusion(bf16[2816,4096]{1,0:T(8,128)(2,1)} %bitcast_select_fusion, bf16[2816,256]{1,0:T(8,128)(2,1)S(1)} %bitcast_select_fusion.1, bf16[128,4096]{1,0:T(8,128)(2,1)S(1)} %get-tuple-element.38, bf16[128,4096]{1,0:T(8,128)(2,1)S(1)} %convolution_convert_fusion), kind=kOutput, calls=%fused_computation.4 | convolution fusion | flops 5944377344 | bytes 49676288 | tf_op jit(solution)/shard_map/dot_general | solution.py:33
  (14 shorter events, 0.2 us)
Async XLA Ops:
  7.2 42.2 %all-gather.4.cloned.1.call-start = ((), (), s32[]{:S(2)}) async-start(), calls=%async_computation | async-start | bytes 1966080 | tf_op jit(solution)/shard_map/all_gather | solution.py:15
  7.9 70.0 %all-gather.6.cloned.1.call-start = ((), (), s32[]{:S(2)}) async-start(), calls=%async_computation.2 | async-start | bytes 1179648 | tf_op jit(solution)/shard_map/all_gather | solution.py:21
  53.2 109.6 %all-reduce.3.cloned.1.call-start = ((), (), s32[]{:S(2)}) async-start(), calls=%async_computation.1 | async-start | bytes 8388608 | tf_op jit(solution)/shard_map/psum | solution.py:28
  140.2 30.2 %copy-start.1 = (f32[2,128,128]{1,2,0:T(8,128)}, f32[2,128,128]{1,2,0:T(8,128)S(1)}, u32[]{:S(2)}) copy-start(f32[2,128,128]{1,2,0:T(8,128)S(1)} %custom-call.19) | copy-start | bytes 393220
  162.8 3.7 %copy-start = (f32[256,4096]{1,0:T(8,128)S(1)}, f32[256,4096]{1,0:T(8,128)}, u32[]{:S(2)}) copy-start(f32[256,4096]{1,0:T(8,128)} %all-reduce.3.cloned.1.call-done) | copy-start | bytes 12582916
  174.8 2.0 copy-start.2
Sparse Core Ops, SparseCore 0:
  9.5 39.7 all-gather.3
  53.4 24.4 all-gather.5
  81.7 81.0 all-reduce.2
